TPU v7x, 512 devices: a whole 4x4x16 slice. The times are simulated.
512 devices in a mesh: section: 16 (over x, y_hi, core), ctx: 32 (over z, y_lo).
Axes of the slice: x: 4, y: 4 (y_hi: 2, y_lo: 2; y = y_hi * 2 + y_lo), z: 16, core: 2. Of those that a mesh axis runs over, the one named last changes fastest.
Arguments:
- queries: bfloat16 [16, 4096, 4096], P('section', 'ctx'), may hold values from -8 to 8
- keys: bfloat16 [16, 4096, 512], P('section', 'ctx'), may hold values from -8 to 8
- values: bfloat16 [16, 4096, 512], P('section', 'ctx'), may hold values from -6 to 6
- token_pos: int32 [4096], P('ctx'), may hold values from 0 to 4095, as said below
- segment: int32 [4096], replicated, may hold values from 0 to 7, never falling along the last dimension, each value on 1 to 1024 neighbouring positions
Outputs:
- handed: bfloat16 [16, 4096, 4096], P('section', 'ctx')
Inputs may be any that keep to these rules, and one draw needn't show every extreme that they name: `token_pos`: a permutation of the 4096 positions; the 128 rows of one index of ctx are two runs of 64 consecutive positions, starting at b * 64 and at (63 - b) * 64, each b used by one index. `segment`: document numbers never fall along the positions; each document covers 1 to 1024 positions, one exactly that many.
All inputs are finite; a program needn't handle non-finite values.
Results may differ from a plain program's by a relative error of at most 0.0059.
Values may be sent and summed in bfloat16 or wider, within the bound.
A program may use at most 64 MiB of HBM per device.

v0:
```python
import math

import jax
import jax.numpy as jnp
from jax import lax
from jax.sharding import PartitionSpec as P

HEAD_SIZE = 128
QUERY_HEADS = 32
KEY_VALUE_HEADS = 4


large_negative_fill = -1e30


def from_behind(x, axis, by):
    size = lax.axis_size(axis)
    return lax.ppermute(x, axis, [(i, (i + by) % size) for i in range(size)])


def tile_update(
    partial_value,
    query_half,
    half_pos,
    half_doc,
    key_block,
    value_block,
    block_pos,
    block_doc,
    inv_scale,
):
    running_max, row_total, weighted = partial_value
    scores = (
        jnp.einsum("hgqd,khd->hgqk", query_half, key_block, preferred_element_type=jnp.float32)
        * inv_scale
    )
    allowed = (block_pos[None, :] <= half_pos[:, None]) & (block_doc[None, :] == half_doc[:, None])
    scores = jnp.where(allowed, scores, large_negative_fill)
    new_max = jnp.maximum(running_max, jnp.max(scores, axis=-1))
    probabilities = jnp.where(allowed, jnp.exp(scores - new_max[..., None]), 0.0)
    factor = jnp.exp(running_max - new_max)
    new_total = row_total * factor + jnp.sum(probabilities, axis=-1)
    new_weighted = weighted * factor[..., None] + jnp.einsum(
        "hgqk,khd->hgqd",
        probabilities.astype(jnp.bfloat16),
        value_block,
        preferred_element_type=jnp.float32,
    )
    return (new_max, new_total, new_weighted)


def visit_keys(carried, incoming, query_split, pos_split, doc_split, all_pos, segment, inv_scale):
    key_rows, value_rows = incoming
    key_count = key_rows.shape[0]
    token_rows = 2 * query_split[0].shape[2]
    rows_per_block = 2 * token_rows
    block_count = key_count // rows_per_block

    def one_block(block_index, state):
        offset_rows = block_index * rows_per_block
        key_block = lax.dynamic_slice_in_dim(key_rows, offset_rows, rows_per_block, 0).reshape(
            rows_per_block, KEY_VALUE_HEADS, HEAD_SIZE
        )
        value_block = lax.dynamic_slice_in_dim(value_rows, offset_rows, rows_per_block, 0).reshape(
            rows_per_block, KEY_VALUE_HEADS, HEAD_SIZE
        )
        block_pos = lax.dynamic_slice_in_dim(all_pos, offset_rows, rows_per_block, 0)
        block_doc = jnp.take(segment, block_pos)
        updated_list = []
        for which_half in range(2):
            is_live = (
                (jnp.min(block_pos) <= jnp.max(pos_split[which_half]))
                & (jnp.min(block_doc) <= jnp.max(doc_split[which_half]))
                & (jnp.max(block_doc) >= jnp.min(doc_split[which_half]))
            )

            def compute_tile(partial_value, which_half=which_half):
                return tile_update(
                    partial_value,
                    query_split[which_half],
                    pos_split[which_half],
                    doc_split[which_half],
                    key_block,
                    value_block,
                    block_pos,
                    block_doc,
                    inv_scale,
                )

            def keep_tile(partial_value):
                return partial_value

            updated_list.append(lax.cond(is_live, compute_tile, keep_tile, state[which_half]))
        return (updated_list[0], updated_list[1])

    return lax.fori_loop(0, block_count, one_block, carried)


def per_device(queries, keys, values, token_pos, segment):
    token_rows = queries.shape[1]
    rows_per_half = token_rows // 2
    query_group_count = QUERY_HEADS // KEY_VALUE_HEADS
    inv_scale = 1.0 / math.sqrt(HEAD_SIZE)
    all_pos = lax.all_gather(token_pos, "ctx", axis=0, tiled=True)
    own_doc = jnp.take(segment, token_pos)
    reshaped_tensor = (
        queries[0]
        .reshape(token_rows, KEY_VALUE_HEADS, query_group_count, HEAD_SIZE)
        .transpose(1, 2, 0, 3)
    )
    query_split = (reshaped_tensor[:, :, :rows_per_half], reshaped_tensor[:, :, rows_per_half:])
    pos_split = (token_pos[:rows_per_half], token_pos[rows_per_half:])
    doc_split = (own_doc[:rows_per_half], own_doc[rows_per_half:])
    blank_state = (
        jnp.full(
            (KEY_VALUE_HEADS, query_group_count, rows_per_half), large_negative_fill, jnp.float32
        ),
        jnp.zeros((KEY_VALUE_HEADS, query_group_count, rows_per_half), jnp.float32),
        jnp.zeros((KEY_VALUE_HEADS, query_group_count, rows_per_half, HEAD_SIZE), jnp.float32),
    )
    initial = (blank_state, blank_state)
    all_keys, all_values = (
        lax.all_gather(keys[0], "ctx", axis=0, tiled=True),
        lax.all_gather(values[0], "ctx", axis=0, tiled=True),
    )
    final = visit_keys(
        initial,
        (all_keys, all_values),
        query_split,
        pos_split,
        doc_split,
        all_pos,
        segment,
        inv_scale,
    )
    normed = []
    for partial_value in final:
        running_max, row_total, weighted = partial_value
        normed.append(weighted / row_total[..., None])
    combined = jnp.concatenate(normed, axis=2)
    attended = (
        combined.transpose(2, 0, 1, 3)
        .reshape(token_rows, QUERY_HEADS * HEAD_SIZE)
        .astype(jnp.bfloat16)[None]
    )
    attended = from_behind(attended, "section", 1)
    return attended


def solution(mesh):
    return jax.shard_map(
        per_device,
        mesh=mesh,
        in_specs=(
            P("section", "ctx", None),
            P("section", "ctx", None),
            P("section", "ctx", None),
            P("ctx"),
            P(),
        ),
        out_specs=P("section", "ctx", None),
        check_vma=False,
    )
```

profile of v0, /device:TPU:8, one launch (start us, length us, event | category | flops | bytes accessed | tf_op | source)
XLA Modules:
  0.0 649.9 jit_solution(4855801955442677882)
XLA Ops:
  6.5 1.7 copy.21
  8.3 1.7 copy.22
  10.0 1.6 copy.23
  14.1 65.5 %all-gather.2 = s32[32,1,128]{2,1,0:T(1,128)S(1)} all-gather(s32[1,1,128]{2,1,0:T(1,128)S(1)} %bitcast.51), channel_id=1, replica_groups=mesh['section'=16,'ctx'=32] {'ctx'}, dimensions={0}, use_global_device_ids=true | all-gather | bytes 16896 | tf_op jit(solution)/shard_map/all_gather | solution.py:104
  80.4 94.5 %all-gather.6.cloned.1.call-done = bf16[1,4096,512]{1,2,0:T(8,128)(2,1)} async-done(((bf16[1,128,512]{1,2,0:T(8,128)(2,1)}), bf16[1,4096,512]{1,2,0:T(8,128)(2,1)}) %all-gather.6.cloned.1.call-update) | async-done | bytes 4194320 | tf_op jit(solution)/shard_map/all_gather | solution.py:123
  175.0 164.4 %all-gather.8.cloned.1.call-done = bf16[1,4096,512]{1,2,0:T(8,128)(2,1)} async-done(((bf16[1,128,512]{1,2,0:T(8,128)(2,1)}), bf16[1,4096,512]{1,2,0:T(8,128)(2,1)}) %all-gather.8.cloned.1.call-update) | async-done | bytes 4194320 | tf_op jit(solution)/shard_map/all_gather | solution.py:124
  340.6 278.9 %while.24 = (s32[]{:T(128)}, f32[4,8,64]{2,1,0:T(8,128)S(1)}, f32[4,8,64]{2,1,0:T(8,128)S(1)}, f32[4,8,64,128]{3,2,1,0:T(8,128)}, f32[4,8,64]{2,1,0:T(8,128)S(1)...) while((s32[]{:T(128)}, f32[4,8,64]{2,1,0:T(8,128)S(1)}, ...), condition=%wide.region_18.19_spmd, body=%wide.region_6.18_spmd.sunk | while | flops 551661824 | bytes 28724928 | solution.py:96
  340.7 1.7 gather_fusion
  351.6 3.8 conditional.4
  355.4 2.8 conditional.5
  357.0 1.2 convolution_add_fusion.1
  358.4 1.7 gather_fusion
  369.2 3.8 conditional.4
  373.1 2.8 conditional.5
  376.0 1.7 gather_fusion
  386.9 3.8 conditional.4
  390.7 2.8 conditional.5
  392.3 1.2 convolution_add_fusion.1
  393.7 1.7 gather_fusion
  404.6 3.8 conditional.4
  408.4 2.8 conditional.5
  411.4 1.7 gather_fusion
  422.2 3.8 conditional.4
  426.1 2.8 conditional.5
  427.7 1.2 convolution_add_fusion.1
  429.0 1.7 gather_fusion
  439.9 3.8 conditional.4
  443.8 2.8 conditional.5
  446.7 1.7 gather_fusion
  457.6 3.8 conditional.4
  461.4 2.8 conditional.5
  463.0 1.2 convolution_add_fusion.1
  464.4 1.7 gather_fusion
  475.3 3.8 conditional.4
  479.1 2.8 conditional.5
  482.1 1.7 gather_fusion
  492.9 3.8 conditional.4
  496.8 2.8 conditional.5
  498.4 1.2 convolution_add_fusion.1
  499.7 1.7 gather_fusion
  510.6 3.8 conditional.4
  514.4 2.8 conditional.5
  517.4 1.7 gather_fusion
  528.3 3.8 conditional.4
  532.1 2.8 conditional.5
  533.7 1.2 convolution_add_fusion.1
  535.1 1.7 gather_fusion
  545.9 3.8 conditional.4
  549.8 2.8 conditional.5
  552.7 1.7 gather_fusion
  563.6 2.9 conditional.5
  565.3 1.2 convolution_add_fusion.1
  566.6 1.7 gather_fusion
  577.5 3.8 conditional.4
  581.3 2.8 conditional.5
  584.3 1.7 gather_fusion
  595.2 3.8 conditional.4
  599.0 2.8 conditional.5
  600.6 1.2 convolution_add_fusion.1
  602.0 1.7 gather_fusion
  612.8 3.8 conditional.4
  616.7 2.8 conditional.5
  622.4 1.9 collective-permute-start
  624.3 17.8 %collective-permute-done = bf16[1,128,4096]{2,1,0:T(8,128)(2,1)S(1)} collective-permute-done((bf16[1,128,4096]{2,1,0:T(8,128)(2,1)S(1)}, bf16[1,128,4096]{2,1,0:T(8,128)(2,1)S(1)}, u32[]{:S(2)}, u32[]{:S(2)}) %collective-permute-start) | collective-permute-done | bytes 1048608 | tf_op jit(solution)/shard_map/ppermute | solution.py:18
  (364 shorter events, 128.4 us)
Async XLA Ops:
  6.5 168.4 %all-gather.6.cloned.1.call-start = ((), (), s32[]{:S(2)}) async-start(), calls=%async_computation | async-start | bytes 4325376 | tf_op jit(solution)/shard_map/all_gather | solution.py:123
  8.2 331.2 %all-gather.8.cloned.1.call-start = ((), (), s32[]{:S(2)}) async-start(), calls=%async_computation.1 | async-start | bytes 4325376 | tf_op jit(solution)/shard_map/all_gather | solution.py:124
  12.1 0.8 copy-start.4
  12.1 0.8 copy-start
  351.7 1.5 copy-start.1
  354.4 1.0 copy-start.2
  369.3 1.5 copy-start.1
  372.1 1.0 copy-start.2
  387.0 1.5 copy-start.1
  389.8 1.0 copy-start.2
  404.7 1.5 copy-start.1
  407.4 1.0 copy-start.2
  422.4 1.5 copy-start.1
  425.1 1.0 copy-start.2
  440.0 1.5 copy-start.1
  442.8 1.0 copy-start.2
  457.7 1.5 copy-start.1
  460.5 1.0 copy-start.2
  475.4 1.5 copy-start.1
  478.1 1.0 copy-start.2
  493.0 1.5 copy-start.1
  495.8 1.0 copy-start.2
  510.7 1.5 copy-start.1
  513.5 1.0 copy-start.2
  528.4 1.5 copy-start.1
  531.1 1.0 copy-start.2
  546.1 1.5 copy-start.1
  548.8 1.0 copy-start.2
  577.6 1.5 copy-start.1
  580.4 1.0 copy-start.2
  595.3 1.5 copy-start.1
  598.0 1.0 copy-start.2
  612.9 1.5 copy-start.1
  615.7 1.0 copy-start.2
  619.5 1.2 copy-start.3
  622.4 19.7 %collective-permute-start = (bf16[1,128,4096]{2,1,0:T(8,128)(2,1)S(1)}, bf16[1,128,4096]{2,1,0:T(8,128)(2,1)S(1)}, u32[]{:S(2)}, u32[]{:S(2)}) collective-permute-start(bf16[1,128,4096]{2,1,0:T(8,128)(2,1)S(1)} %convert_element_type.37), channel_id=1, source_target_pairs={{0,32},{32,64},{64,96},{96,128},{128,160},{160,192},{192,224},{224... | collective-permute-start | bytes 3145736 | tf_op jit(solution)/shard_map/ppermute | solution.py:18
Sparse Core Ops, SparseCore 0:
  9.4 165.5 all-gather.5
  177.0 162.3 all-gather.7
where the time goes:
time: 652 us; the launch traced here: 650 us
  waiting for transfers between devices  277 us (42%)
  loops' own time  122 us (19%)
  local copies, waits for them, and re-layouts  70.8 us (11%)
  blocking collectives  65.5 us (10%)
  matrix products  54.1 us (8%)
  other arithmetic  45.7 us (7%)
  between operations  13.6 us (2%)
    all_gather x1, waiting for transfers between devices, per_device(): lax.all_gather(values[0], 'ctx', axis=0, tiled=True)  164 us
    another operation x1, loops' own time, visit_keys(): return lax.fori_loop(0, block_count, one_block, carried)  119 us
    all_gather x1, waiting for transfers between devices, per_device(): lax.all_gather(keys[0], 'ctx', axis=0, tiled=True)  94.5 us
    all_gather x1, blocking collectives, per_device(): all_pos = lax.all_gather(token_pos, 'ctx', axis=0, tiled=True)  65.5 us
    dot_general x31, matrix products, tile_update(): jnp.einsum('hgqk,khd->hgqd', probabilities.astype(jnp.bfloat16), value_bl...  38 us
    reduce_sum x31, other arithmetic, tile_update(): new_total = row_total * factor + jnp.sum(probabilities, axis=-1)  29.1 us
    gather x16, local copies, waits for them, and re-layouts, one_block(): block_doc = jnp.take(segment, block_pos)  27.5 us
    ppermute x1, waiting for transfers between devices, from_behind(): return lax.ppermute(x, axis, [(i, (i + by) % size) for i in range(size)])  17.8 us
  transfers between devices with their start and end apart: 3, of which 3 were waited for; matrix products, arithmetic and copies ran while one was open for 1% of the time, Pallas kernels for 0%

commit v1 on v0

v1 whole, which is shorter than its diff:
```python
import functools
import math

import jax
import jax.numpy as jnp
from jax import lax
from jax.experimental import pallas as pl
from jax.experimental.pallas import tpu as pltpu
from jax.sharding import PartitionSpec as P

HEAD_SIZE = 128
QUERY_HEADS = 32
KEY_VALUE_HEADS = 4
DOCS = 8
GROUP = QUERY_HEADS // KEY_VALUE_HEADS
STAGES = KEY_VALUE_HEADS // 2
ROWS = 128
WIDE = GROUP * HEAD_SIZE
NEG = -1e30
MESH = pl.DeviceIdType.MESH


def kernel(
    sections,
    ring,
    q_hbm,
    k_hbm,
    v_hbm,
    pos_ref,
    seg_ref,
    out_hbm,
    kv,
    qbuf,
    obuf,
    posbuf,
    qrow,
    bias,
    vt,
    acc,
    top,
    total,
    loc_sem,
    par_send,
    par_recv,
    ring_send,
    ring_recv,
    pos_send,
    pos_recv,
    out_send,
    out_recv,
):
    groups = ring
    last = groups - 1
    sec = lax.axis_index("section")
    ctx = lax.axis_index("ctx")
    half = lax.rem(ctx, 2)
    mate = ctx + 1 - 2 * half
    right = lax.rem(ctx + 2, 2 * ring)
    left = lax.rem(ctx + 2 * ring - 2, 2 * ring)
    onward = lax.rem(sec + 1, sections)
    behind = lax.rem(sec + sections - 1, sections)
    toward = ((sec, right), (sec, left))

    def head_cols(which_half, stage):
        return pl.ds(pl.multiple_of((STAGES * which_half + stage) * HEAD_SIZE, HEAD_SIZE), HEAD_SIZE)

    def wide_cols(which_half, stage):
        return pl.ds(pl.multiple_of((STAGES * which_half + stage) * WIDE, WIDE), WIDE)

    local = []
    for stage in range(STAGES):
        local.append(
            (
                pltpu.make_async_copy(
                    k_hbm.at[0, :, head_cols(half, stage)], kv.at[stage, 0, 0, 0], loc_sem.at[stage, 0]
                ),
                pltpu.make_async_copy(
                    v_hbm.at[0, :, head_cols(half, stage)], kv.at[stage, 0, 1, 0], loc_sem.at[stage, 1]
                ),
                pltpu.make_async_copy(
                    q_hbm.at[0, :, wide_cols(half, stage)],
                    qbuf.at[stage, pl.ds(0, ROWS), :],
                    loc_sem.at[stage, 2],
                ),
            )
        )
    for copies in local:
        for copy in copies:
            copy.start()
    posbuf[0] = pos_ref[...].astype(jnp.float32)

    def swap(stage):
        return (
            pltpu.make_async_remote_copy(
                k_hbm.at[0, :, head_cols(1 - half, stage)],
                kv.at[stage, 0, 0, 1],
                par_send.at[stage, 0],
                par_recv.at[stage, 0],
                device_id=(sec, mate),
                device_id_type=MESH,
            ),
            pltpu.make_async_remote_copy(
                v_hbm.at[0, :, head_cols(1 - half, stage)],
                kv.at[stage, 0, 1, 1],
                par_send.at[stage, 1],
                par_recv.at[stage, 1],
                device_id=(sec, mate),
                device_id_type=MESH,
            ),
            pltpu.make_async_remote_copy(
                q_hbm.at[0, :, wide_cols(1 - half, stage)],
                qbuf.at[stage, pl.ds(ROWS, ROWS), :],
                par_send.at[stage, 2],
                par_recv.at[stage, 2],
                device_id=(sec, mate),
                device_id_type=MESH,
            ),
        )

    def ring_copy(stage, from_group, from_side, group, way):
        return pltpu.make_async_remote_copy(
            kv.at[stage, from_group, :, from_side],
            kv.at[stage, group, :, way],
            ring_send.at[stage, group, way],
            ring_recv.at[stage, group, way],
            device_id=toward[way],
            device_id_type=MESH,
        )

    def pos_copy(from_slot, group, way, device):
        slot = 2 * group + way
        return pltpu.make_async_remote_copy(
            posbuf.at[from_slot],
            posbuf.at[slot],
            pos_send.at[slot],
            pos_recv.at[slot],
            device_id=device,
            device_id_type=MESH,
        )

    mate_pos = pos_copy(0, 0, 1, (sec, mate))

    barrier = pltpu.get_barrier_semaphore()
    greeted = (
        (sec, mate),
        (sec, right),
        (sec, left),
        (onward, ctx),
        (onward, mate),
        (behind, ctx),
        (behind, mate),
    )
    for device in greeted:
        pl.semaphore_signal(barrier, inc=1, device_id=device, device_id_type=MESH)
    pl.semaphore_wait(barrier, len(greeted))

    swap_a = swap(0)
    swap_a[0].start()
    swap_a[1].start()
    mate_pos.start()

    def launch(stage, side):
        for way in range(2):
            ring_copy(stage, 0, side, 1 + side, way).start()
            if stage == 0:
                pos_copy(side, 1 + side, way, toward[way]).start()

    def arrive(stage, group, way):
        ring_copy(stage, 0, 0, group, way).wait_recv()
        if stage == 0:
            pos_copy(0, group, way, toward[way]).wait_recv()

    def pass_on(stage, group, into, way):
        ring_copy(stage, group, way, into, way).start()
        if stage == 0:
            pos_copy(2 * group + way, into, way, toward[way]).start()

    def take(stage, group):
        arrive(stage, group, 0)
        if isinstance(group, int):
            if group <= last - 2:
                pass_on(stage, group, group + 2, 0)
        else:
            pass_on(stage, group, group + 2, 0)
        arrive(stage, group, 1)
        if isinstance(group, int):
            if group <= last - 3:
                pass_on(stage, group, group + 2, 1)
            elif group == last - 1:
                pass_on(stage, group, last, 1)
        else:
            pass_on(stage, group, group + 2, 1)

    local[0][0].wait()
    local[0][1].wait()
    launch(0, 0)
    swap_a[2].start()
    swap_a[0].wait_recv()
    swap_a[1].wait_recv()
    mate_pos.wait_recv()
    launch(0, 1)

    place = jnp.concatenate([posbuf[0], posbuf[1]], axis=1)
    first = jnp.zeros_like(place)
    for doc in range(1, DOCS):
        count = jnp.sum((seg_ref[...] < doc).astype(jnp.float32), axis=0, keepdims=True)
        begin = jnp.sum(count, axis=1, keepdims=True)
        first = jnp.maximum(first, jnp.where(begin <= place, begin, 0.0))
    qrow[0] = place
    qrow[1] = first

    scale = math.log2(math.e) / math.sqrt(HEAD_SIZE)

    def attend(stage, group, finish=False):
        for way in range(2):
            spot = jnp.transpose(jnp.broadcast_to(posbuf[2 * group + way], (ROWS, ROWS)))
            for side in range(2):
                lanes = slice(side * ROWS, (side + 1) * ROWS)
                allowed = (spot <= qrow[0, :, lanes]) & (spot >= qrow[1, :, lanes])
                bias[way * ROWS : (way + 1) * ROWS, lanes] = jnp.where(allowed, 0.0, NEG)
            vt[:, way * ROWS : (way + 1) * ROWS] = jnp.transpose(kv[stage, group, 1, way])
        key_rows = kv[stage, group, 0].reshape(2 * ROWS, HEAD_SIZE)
        for head in range(GROUP):
            cols = slice(head * HEAD_SIZE, (head + 1) * HEAD_SIZE)
            scores = lax.dot_general(
                key_rows,
                qbuf[stage, :, cols],
                (((1,), (1,)), ((), ())),
                preferred_element_type=jnp.float32,
            )
            scores = scores * scale + bias[...]
            old = top[head]
            new = jnp.maximum(old, jnp.max(scores, axis=0, keepdims=True))
            probabilities = jnp.exp2(scores - new)
            factor = jnp.exp2(old - new)
            row_total = total[head] * factor + jnp.sum(probabilities, axis=0, keepdims=True)
            weighted = acc[head] * factor + jnp.dot(
                vt[...], probabilities.astype(jnp.bfloat16), preferred_element_type=jnp.float32
            )
            if finish:
                result = jnp.transpose(weighted * (1.0 / row_total))
                obuf[stage, :, cols] = result.astype(jnp.bfloat16)
                for side in range(2):
                    hand(stage, head, side).start()
            else:
                top[head] = new
                total[head] = row_total
                acc[head] = weighted

    def hand(stage, head, side):
        spot = pl.multiple_of(((STAGES * half + stage) * GROUP + head) * HEAD_SIZE, HEAD_SIZE)
        return pltpu.make_async_remote_copy(
            obuf.at[stage, pl.ds(side * ROWS, ROWS), pl.ds(head * HEAD_SIZE, HEAD_SIZE)],
            out_hbm.at[0, :, pl.ds(spot, HEAD_SIZE)],
            out_send.at[stage, head, side],
            out_recv.at[stage, head, side],
            device_id=(onward, ctx if side == 0 else mate),
            device_id_type=MESH,
        )

    def start_stage():
        top[...] = jnp.full_like(top, NEG)
        total[...] = jnp.zeros_like(total)
        acc[...] = jnp.zeros_like(acc)

    swap_b = swap(1)

    start_stage()
    idle = min(5, last - 3)
    pairs = max(0, min(last - 3, 2 * idle + 1) - idle)

    def passing(group, carry):
        take(0, group)
        return carry

    lax.fori_loop(1, idle + 1, passing, 0)
    for copy in swap_b:
        copy.start()
    local[0][2].wait()
    swap_a[2].wait_recv()

    def catching_up(group, carry):
        take(0, group)

        def one(index, carry):
            attend(0, 2 * (group - idle - 1) + index)
            return carry

        return lax.fori_loop(0, 2, one, carry)

    lax.fori_loop(idle + 1, idle + pairs + 1, catching_up, 0)
    done = 2 * pairs
    local[1][0].wait()
    local[1][1].wait()

    def working(stage):
        def step(group, carry):
            attend(stage, group)
            return carry

        return step

    for group in range(idle + pairs + 1, last + 1):
        take(0, group)
        if group == last - 2:
            launch(1, 0)
        if group == last - 1:
            swap_b[0].wait_recv()
            swap_b[1].wait_recv()
            launch(1, 1)
        until = min(group + 1, last)
        lax.fori_loop(done, until, working(0), 0)
        done = until
    attend(0, last, finish=True)

    start_stage()
    local[1][2].wait()
    swap_b[2].wait_recv()

    def both(group, carry):
        attend(1, group)
        take(1, group + 1)
        return carry

    lax.fori_loop(0, last - 3, both, 0)
    for group in range(last - 3, last):
        lax.fori_loop(group, group + 1, working(1), 0)
        take(1, group + 1)
    attend(1, last, finish=True)

    for copy in swap_a + swap_b + (mate_pos,):
        copy.wait_send()

    def sent(group, carry):
        for way in range(2):
            for stage in range(STAGES):
                ring_copy(stage, 0, 0, group, way).wait_send()
            pos_copy(0, group, way, toward[way]).wait_send()
        return carry

    lax.fori_loop(1, groups, sent, 0)

    for stage in range(STAGES):
        for head in range(GROUP):
            for side in range(2):
                copy = hand(stage, head, side)
                copy.wait_send()
                copy.wait_recv()


def per_device(sections, ring, queries, keys, values, token_pos, segment):
    anywhere = pl.BlockSpec(memory_space=pl.ANY)
    inside = pl.BlockSpec(memory_space=pltpu.VMEM)
    dma = pltpu.SemaphoreType.DMA
    pairs = ROWS * 2 * ring * ROWS * 2 * QUERY_HEADS // 2
    return pl.pallas_call(
        functools.partial(kernel, sections, ring),
        out_shape=jax.ShapeDtypeStruct(queries.shape, jnp.bfloat16),
        in_specs=[anywhere, anywhere, anywhere, inside, inside],
        out_specs=anywhere,
        scratch_shapes=[
            pltpu.VMEM((STAGES, ring, 2, 2, ROWS, HEAD_SIZE), jnp.bfloat16),
            pltpu.VMEM((STAGES, 2 * ROWS, WIDE), jnp.bfloat16),
            pltpu.VMEM((STAGES, 2 * ROWS, WIDE), jnp.bfloat16),
            pltpu.VMEM((2 * ring, 1, ROWS), jnp.float32),
            pltpu.VMEM((2, 1, 2 * ROWS), jnp.float32),
            pltpu.VMEM((2 * ROWS, 2 * ROWS), jnp.float32),
            pltpu.VMEM((HEAD_SIZE, 2 * ROWS), jnp.bfloat16),
            pltpu.VMEM((GROUP, HEAD_SIZE, 2 * ROWS), jnp.float32),
            pltpu.VMEM((GROUP, 1, 2 * ROWS), jnp.float32),
            pltpu.VMEM((GROUP, 1, 2 * ROWS), jnp.float32),
            dma((STAGES, 3)),
            dma((STAGES, 3)),
            dma((STAGES, 3)),
            dma((STAGES, ring, 2)),
            dma((STAGES, ring, 2)),
            dma((2 * ring,)),
            dma((2 * ring,)),
            dma((STAGES, GROUP, 2)),
            dma((STAGES, GROUP, 2)),
        ],
        compiler_params=pltpu.CompilerParams(
            collective_id=0, has_side_effects=True, vmem_limit_bytes=48 * 1024 * 1024
        ),
        cost_estimate=pl.CostEstimate(
            flops=4 * HEAD_SIZE * pairs, bytes_accessed=4 * 1024 * 1024, transcendentals=pairs
        ),
    )(queries, keys, values, token_pos.reshape(1, ROWS), segment.reshape(-1, 128))


def solution(mesh):
    return jax.shard_map(
        functools.partial(per_device, mesh.shape["section"], mesh.shape["ctx"] // 2),
        mesh=mesh,
        in_specs=(
            P("section", "ctx", None),
            P("section", "ctx", None),
            P("section", "ctx", None),
            P("ctx"),
            P(),
        ),
        out_specs=P("section", "ctx", None),
        check_vma=False,
    )
```

time: 652 us -> 122 us (0.19)
  the two profiles are of different devices: /device:TPU:8 before, /device:TPU:1 now
where the time goes in v1:
time: 122 us
  Pallas kernels  117 us (96%)
  local copies, waits for them, and re-layouts  5.38 us (4%)
    pallas_call x1, Pallas kernels, per_device(): pl.pallas_call(functools.partial(kernel, sections, ring), out_shape=jax.S...  117 us
    unnamed x11, local copies, waits for them, and re-layouts  5.38 us

profile of v1, /device:TPU:1, one launch (start us, length us, event | category | flops | bytes accessed | tf_op | source)
XLA Modules:
  0.0 122.0 jit_solution(2964718010024243761)
XLA Ops:
  0.0 0.0 copy-start.4
  0.0 0.7 copy-done.4
  0.7 0.0 copy-start
  0.7 1.2 %copy-done = bf16[1,128,4096]{2,1,0:T(8,128)(2,1)S(1)} copy-done((bf16[1,128,4096]{2,1,0:T(8,128)(2,1)S(1)}, bf16[1,128,4096]{2,1,0:T(8,128)(2,1)}, u32[]{:S(2)}) %copy-start) | copy-done | bytes 1048600
  1.9 0.0 copy-start.1
  1.9 0.9 copy-done.1
  2.8 0.0 copy-start.2
  2.8 0.9 copy-done.2
  3.7 0.0 copy-start.3
  3.7 0.7 copy-done.3
  4.4 116.6 %shard_map.55 = bf16[1,128,4096]{2,1,0:T(8,128)(2,1)S(1)} custom-call(bf16[1,128,4096]{2,1,0:T(8,128)(2,1)S(1)} %copy-done, bf16[1,128,512]{2,1,0:T(8,128)(2,1)S(1)} %copy-done.1, bf16[1,128,512]{2,1,0:T(8,128)(2,1)S(1)} %copy-done.2, s32[1,128]{1,0:T(1,128)S(1)} %bitcast.3, s32[32,128]{1,0:T(8,128)S(1)} %bitcast.2), custom_call_target="tpu_custom_call" | custom-call | flops 8589934592 | bytes 4194304 | tf_op jit(solution)/shard_map/pallas_call | solution.py:356
  121.0 1.0 copy.7
Async XLA Ops:
  0.0 0.7 copy-start.4
  0.7 1.2 %copy-start = (bf16[1,128,4096]{2,1,0:T(8,128)(2,1)S(1)}, bf16[1,128,4096]{2,1,0:T(8,128)(2,1)}, u32[]{:S(2)}) copy-start(bf16[1,128,4096]{2,1,0:T(8,128)(2,1)} %q_hbm.1) | copy-start | bytes 3145732
  1.9 0.9 copy-start.1
  2.8 0.9 copy-start.2
  3.7 0.7 copy-start.3

commit v2 on v1

v2 whole, which is shorter than its diff:
```python
import functools
import math

import jax
import jax.numpy as jnp
from jax import lax
from jax.experimental import pallas as pl
from jax.experimental.pallas import tpu as pltpu
from jax.sharding import PartitionSpec as P

HEAD_SIZE = 128
QUERY_HEADS = 32
KEY_VALUE_HEADS = 4
DOCS = 8
GROUP = QUERY_HEADS // KEY_VALUE_HEADS
STAGES = KEY_VALUE_HEADS // 2
ROWS = 128
WIDE = GROUP * HEAD_SIZE
NEG = -1e30
MESH = pl.DeviceIdType.MESH


def kernel(
    sections,
    ring,
    q_hbm,
    k_hbm,
    v_hbm,
    pos_hbm,
    seg_hbm,
    out_hbm,
    kv,
    qbuf,
    obuf,
    pos_ref,
    seg_ref,
    posbuf,
    qrow,
    bias,
    vt,
    acc,
    top,
    total,
    loc_sem,
    par_send,
    par_recv,
    ring_send,
    ring_recv,
    pos_send,
    pos_recv,
    out_send,
    out_recv,
):
    hops = ring // 2
    sec = lax.axis_index("section")
    ctx = lax.axis_index("ctx")
    half = lax.rem(ctx, 2)
    mate = ctx + 1 - 2 * half
    right = lax.rem(ctx + 2, 2 * ring)
    left = lax.rem(ctx + 2 * ring - 2, 2 * ring)
    onward = lax.rem(sec + 1, sections)
    behind = lax.rem(sec + sections - 1, sections)
    toward = ((sec, right), (sec, left))

    def head_cols(which_half, stage):
        return pl.ds(pl.multiple_of((STAGES * which_half + stage) * HEAD_SIZE, HEAD_SIZE), HEAD_SIZE)

    def wide_cols(which_half, stage):
        return pl.ds(pl.multiple_of((STAGES * which_half + stage) * WIDE, WIDE), WIDE)

    local = []
    for stage in range(STAGES):
        local.append(
            (
                pltpu.make_async_copy(
                    k_hbm.at[0, :, head_cols(half, stage)], kv.at[stage, 0, 0, 0], loc_sem.at[stage, 0]
                ),
                pltpu.make_async_copy(
                    v_hbm.at[0, :, head_cols(half, stage)], kv.at[stage, 0, 1, 0], loc_sem.at[stage, 1]
                ),
                pltpu.make_async_copy(
                    q_hbm.at[0, :, wide_cols(half, stage)],
                    qbuf.at[stage, pl.ds(0, ROWS), :],
                    loc_sem.at[stage, 2],
                ),
            )
        )
    small = (
        pltpu.make_async_copy(pos_hbm, pos_ref, loc_sem.at[0, 3]),
        pltpu.make_async_copy(seg_hbm, seg_ref, loc_sem.at[1, 3]),
    )
    for copy in small + local[0] + local[1]:
        copy.start()
    small[0].wait()
    posbuf[0] = pos_ref[...].astype(jnp.float32)

    def swap(stage):
        return (
            pltpu.make_async_remote_copy(
                k_hbm.at[0, :, head_cols(1 - half, stage)],
                kv.at[stage, 0, 0, 3],
                par_send.at[stage, 0],
                par_recv.at[stage, 0],
                device_id=(sec, mate),
                device_id_type=MESH,
            ),
            pltpu.make_async_remote_copy(
                v_hbm.at[0, :, head_cols(1 - half, stage)],
                kv.at[stage, 0, 1, 3],
                par_send.at[stage, 1],
                par_recv.at[stage, 1],
                device_id=(sec, mate),
                device_id_type=MESH,
            ),
            pltpu.make_async_remote_copy(
                q_hbm.at[0, :, wide_cols(1 - half, stage)],
                qbuf.at[stage, pl.ds(ROWS, ROWS), :],
                par_send.at[stage, 2],
                par_recv.at[stage, 2],
                device_id=(sec, mate),
                device_id_type=MESH,
            ),
        )

    def ring_copy(stage, hop, from_piece, piece):
        return pltpu.make_async_remote_copy(
            kv.at[stage, hop, :, from_piece],
            kv.at[stage, hop + 1, :, piece],
            ring_send.at[stage, hop + 1, piece],
            ring_recv.at[stage, hop + 1, piece],
            device_id=toward[piece % 2],
            device_id_type=MESH,
        )

    def pos_copy(from_slot, slot, device):
        return pltpu.make_async_remote_copy(
            posbuf.at[from_slot],
            posbuf.at[slot],
            pos_send.at[slot],
            pos_recv.at[slot],
            device_id=device,
            device_id_type=MESH,
        )

    mate_pos = pos_copy(0, 3, (sec, mate))

    barrier = pltpu.get_barrier_semaphore()
    greeted = (
        (sec, mate),
        (sec, right),
        (sec, left),
        (onward, ctx),
        (onward, mate),
        (behind, ctx),
        (behind, mate),
    )
    for device in greeted:
        pl.semaphore_signal(barrier, inc=1, device_id=device, device_id_type=MESH)
    pl.semaphore_wait(barrier, len(greeted))

    swap_a = swap(0)
    swap_a[0].start()
    swap_a[1].start()
    mate_pos.start()

    def send(stage, hop, from_piece, piece):
        ring_copy(stage, hop, from_piece, piece).start()

        @pl.when(stage == 0)
        def _():
            pos_copy(4 * hop + from_piece, 4 * hop + 4 + piece, toward[piece % 2]).start()

    def launch(stage, side):
        for way in range(2):
            send(stage, 0, 3 * side, 2 * side + way)

    def take(stage, hop):
        for piece in range(4) if not (isinstance(hop, int) and hop == hops) else (0, 3):
            ring_copy(stage, hop - 1, 0, piece).wait_recv()

            @pl.when(stage == 0)
            def _():
                pos_copy(0, 4 * hop + piece, toward[piece % 2]).wait_recv()

            if isinstance(hop, int):
                if hop < hops - 1 or (hop == hops - 1 and piece in (0, 3)):
                    send(stage, hop, piece, piece)
            elif piece in (0, 3):
                send(stage, hop, piece, piece)
            else:

                @pl.when(hop < hops - 1)
                def _():
                    send(stage, hop, piece, piece)

    local[0][0].wait()
    local[0][1].wait()
    launch(0, 0)
    swap_a[2].start()
    swap_a[0].wait_recv()
    swap_a[1].wait_recv()
    mate_pos.wait_recv()
    launch(0, 1)

    small[1].wait()

    place = jnp.concatenate([posbuf[0], posbuf[3]], axis=1)
    first = jnp.zeros_like(place)
    for doc in range(1, DOCS):
        count = jnp.sum((seg_ref[...] < doc).astype(jnp.float32), axis=0, keepdims=True)
        begin = jnp.sum(count, axis=1, keepdims=True)
        first = jnp.maximum(first, jnp.where(begin <= place, begin, 0.0))
    qrow[0] = place
    qrow[1] = first

    scale = math.log2(math.e) / math.sqrt(HEAD_SIZE)

    def attend(stage, hop, pieces=(0, 1, 2, 3), finish=False):
        width = len(pieces) * ROWS

        @pl.when(stage == 0)
        def _():
            for at, piece in enumerate(pieces):
                spot = jnp.transpose(jnp.broadcast_to(posbuf[4 * hop + piece], (ROWS, ROWS)))
                for side in range(2):
                    lanes = slice(side * ROWS, (side + 1) * ROWS)
                    allowed = (spot <= qrow[0, :, lanes]) & (spot >= qrow[1, :, lanes])
                    bias[hop, at * ROWS : (at + 1) * ROWS, lanes] = jnp.where(allowed, 0.0, NEG)

        for at, piece in enumerate(pieces):
            vt[:, at * ROWS : (at + 1) * ROWS] = jnp.transpose(kv[stage, hop, 1, piece])
        key_rows = jnp.concatenate([kv[stage, hop, 0, piece] for piece in pieces], axis=0)

        def score(head):
            return lax.dot_general(
                key_rows,
                qbuf[stage, :, head * HEAD_SIZE : (head + 1) * HEAD_SIZE],
                (((1,), (1,)), ((), ())),
                preferred_element_type=jnp.float32,
            )

        def soften(head, scores):
            scores = scores * scale + bias[hop, :width]
            old = top[stage, head]
            new = jnp.maximum(old, jnp.max(scores, axis=0, keepdims=True))
            probabilities = jnp.exp2(scores - new)
            factor = jnp.exp2(old - new)
            total[stage, head] = total[stage, head] * factor + jnp.sum(
                probabilities, axis=0, keepdims=True
            )
            top[stage, head] = new
            return probabilities.astype(jnp.bfloat16), factor

        def weigh(head, probabilities, factor):
            weighted = acc[stage, head] * factor + jnp.dot(
                vt[:, :width], probabilities, preferred_element_type=jnp.float32
            )
            if finish:
                result = jnp.transpose(weighted * (1.0 / total[stage, head]))
                obuf[stage, :, head * HEAD_SIZE : (head + 1) * HEAD_SIZE] = result.astype(
                    jnp.bfloat16
                )
                for side in range(2):
                    hand(stage, head, side).start()
            else:
                acc[stage, head] = weighted

        scores, behind_by_one = score(0), None
        for head in range(GROUP):
            following = score(head + 1) if head + 1 < GROUP else None
            softened = soften(head, scores)
            if behind_by_one is not None:
                weigh(head - 1, *behind_by_one)
            scores, behind_by_one = following, softened
        weigh(GROUP - 1, *behind_by_one)

    def hand(stage, head, side):
        spot = pl.multiple_of(((STAGES * half + stage) * GROUP + head) * HEAD_SIZE, HEAD_SIZE)
        return pltpu.make_async_remote_copy(
            obuf.at[stage, pl.ds(side * ROWS, ROWS), pl.ds(head * HEAD_SIZE, HEAD_SIZE)],
            out_hbm.at[0, :, pl.ds(spot, HEAD_SIZE)],
            out_send.at[stage, head, side],
            out_recv.at[stage, head, side],
            device_id=(onward, ctx if side == 0 else mate),
            device_id_type=MESH,
        )

    swap_b = swap(1)
    ends = (0, 3)

    def first_hop_of_b():
        for copy in swap_b:
            copy.start()
        local[1][0].wait()
        local[1][1].wait()
        launch(1, 0)
        swap_b[0].wait_recv()
        swap_b[1].wait_recv()
        launch(1, 1)

    top[...] = jnp.full_like(top, NEG)
    total[...] = jnp.zeros_like(total)
    acc[...] = jnp.zeros_like(acc)
    take(0, 1)
    first_hop_of_b()
    if hops == 8:
        take(0, 2)
        take(1, 1)
        local[0][2].wait()
        swap_a[2].wait_recv()
        attend(0, 0, ends)

        def early(index, carry):
            attend(0, index)
            stage = lax.rem(index + 1, 2)
            take(stage, (index + 5) // 2 - stage)
            return carry

        lax.fori_loop(1, 5, early, 0)
        local[1][2].wait()
        swap_b[2].wait_recv()
        attend(1, 0, ends)

        def late(index, carry):
            turn, which = index // 3, lax.rem(index, 3)
            stage = lax.rem(which + 1, 2)
            attend(stage, stage * (2 * turn + 1 + which // 2) + (1 - stage) * (5 + turn))

            @pl.when(which < 2)
            def _():
                take(which, 5 + turn - which)

            return carry

        lax.fori_loop(0, 9, late, 0)
        take(0, 8)
        take(1, 7)
        attend(0, 8, ends, finish=True)
        attend(1, 7)
        take(1, 8)
        attend(1, 8, ends, finish=True)
    else:
        local[0][2].wait()
        swap_a[2].wait_recv()
        local[1][2].wait()
        swap_b[2].wait_recv()
        for stage in range(STAGES):
            attend(stage, 0, ends)
        take(1, 1)
        for hop in range(1, hops):
            for stage in range(STAGES):
                attend(stage, hop)
                take(stage, hop + 1)
        for stage in range(STAGES):
            attend(stage, hops, ends, finish=True)

    for copy in swap_a + swap_b + (mate_pos,):
        copy.wait_send()

    def sent(hop, pieces):
        for piece in pieces:
            for stage in range(STAGES):
                ring_copy(stage, hop - 1, 0, piece).wait_send()
            pos_copy(0, 4 * hop + piece, toward[piece % 2]).wait_send()

    def all_sent(hop, carry):
        sent(hop, range(4))
        return carry

    lax.fori_loop(1, hops, all_sent, 0)
    sent(hops, ends)

    for stage in range(STAGES):
        for head in range(GROUP):
            for side in range(2):
                copy = hand(stage, head, side)
                copy.wait_send()
                copy.wait_recv()


def per_device(sections, ring, queries, keys, values, token_pos, segment):
    anywhere = pl.BlockSpec(memory_space=pl.ANY)
    dma = pltpu.SemaphoreType.DMA
    hops = ring // 2
    pairs = ROWS * 2 * ring * ROWS * 2 * QUERY_HEADS // 2
    return pl.pallas_call(
        functools.partial(kernel, sections, ring),
        out_shape=jax.ShapeDtypeStruct(queries.shape, jnp.bfloat16),
        in_specs=[anywhere] * 5,
        out_specs=anywhere,
        scratch_shapes=[
            pltpu.VMEM((STAGES, hops + 1, 2, 4, ROWS, HEAD_SIZE), jnp.bfloat16),
            pltpu.VMEM((STAGES, 2 * ROWS, WIDE), jnp.bfloat16),
            pltpu.VMEM((STAGES, 2 * ROWS, WIDE), jnp.bfloat16),
            pltpu.VMEM((1, ROWS), jnp.int32),
            pltpu.VMEM((ring * ROWS * 2 // 128, 128), jnp.int32),
            pltpu.VMEM((4 * hops + 4, 1, ROWS), jnp.float32),
            pltpu.VMEM((2, 1, 2 * ROWS), jnp.float32),
            pltpu.VMEM((hops + 1, 4 * ROWS, 2 * ROWS), jnp.float32),
            pltpu.VMEM((HEAD_SIZE, 4 * ROWS), jnp.bfloat16),
            pltpu.VMEM((STAGES, GROUP, HEAD_SIZE, 2 * ROWS), jnp.float32),
            pltpu.VMEM((STAGES, GROUP, 1, 2 * ROWS), jnp.float32),
            pltpu.VMEM((STAGES, GROUP, 1, 2 * ROWS), jnp.float32),
            dma((STAGES, 4)),
            dma((STAGES, 3)),
            dma((STAGES, 3)),
            dma((STAGES, hops + 1, 4)),
            dma((STAGES, hops + 1, 4)),
            dma((4 * hops + 4,)),
            dma((4 * hops + 4,)),
            dma((STAGES, GROUP, 2)),
            dma((STAGES, GROUP, 2)),
        ],
        compiler_params=pltpu.CompilerParams(
            collective_id=0, has_side_effects=True, vmem_limit_bytes=60 * 1024 * 1024
        ),
        cost_estimate=pl.CostEstimate(
            flops=4 * HEAD_SIZE * pairs, bytes_accessed=4 * 1024 * 1024, transcendentals=pairs
        ),
    )(queries, keys, values, token_pos.reshape(1, ROWS), segment.reshape(-1, 128))


def solution(mesh):
    return jax.shard_map(
        functools.partial(per_device, mesh.shape["section"], mesh.shape["ctx"] // 2),
        mesh=mesh,
        in_specs=(
            P("section", "ctx", None),
            P("section", "ctx", None),
            P("section", "ctx", None),
            P("ctx"),
            P(),
        ),
        out_specs=P("section", "ctx", None),
        check_vma=False,
    )
```

time: 122 us -> 79.1 us (0.65)
  Pallas kernels: 117 us -> 76.7 us
  local copies, waits for them, and re-layouts: 5.38 us -> 2.29 us
    pallas_call x1, Pallas kernels: 117 us -> 76.7 us  [per_device(): pl.pallas_call(functools.partial(kernel, sections, ring), out_shape=jax.S...]
    unnamed x11 -> x1, local copies, waits for them, and re-layouts: 5.38 us -> 2.29 us
where the time goes in v2:
time: 79.1 us; the launch traced here: 79 us
  Pallas kernels  76.7 us (97%)
  local copies, waits for them, and re-layouts  2.29 us (3%)
    pallas_call x1, Pallas kernels, per_device(): pl.pallas_call(functools.partial(kernel, sections, ring), out_shape=jax.S...  76.7 us
    unnamed x1, local copies, waits for them, and re-layouts  2.29 us

profile of v2, /device:TPU:1, one launch (start us, length us, event | category | flops | bytes accessed | tf_op | source)
XLA Modules:
  0.0 79.0 jit_solution(9199319567426048603)
XLA Ops:
  0.0 76.7 %shard_map.55 = bf16[1,128,4096]{2,1,0:T(8,128)(2,1)} custom-call(bf16[1,128,4096]{2,1,0:T(8,128)(2,1)} %q_hbm.1, bf16[1,128,512]{2,1,0:T(8,128)(2,1)} %k_hbm.1, bf16[1,128,512]{2,1,0:T(8,128)(2,1)} %v_hbm.1, s32[1,128]{1,0:T(1,128)} %bitcast.3, s32[32,128]{1,0:T(8,128)} %bitcast.2), custom_call_target="tpu_custom_call" | custom-call | flops 8589934592 | bytes 4194304 | tf_op jit(solution)/shard_map/pallas_call | solution.py:386
  76.7 2.3 %copy.7 = bf16[1,128,4096]{2,1,0:T(8,128)(2,1)} copy(bf16[1,128,4096]{2,1,0:T(8,128)(2,1)} %shard_map.55) | data formatting | bytes 2097152

commit v3 on v2

--- a/solution.py
+++ b/solution.py
@@ -158,10 +158,9 @@
         pl.semaphore_signal(barrier, inc=1, device_id=device, device_id_type=MESH)
     pl.semaphore_wait(barrier, len(greeted))
 
-    swap_a = swap(0)
-    swap_a[0].start()
-    swap_a[1].start()
-    mate_pos.start()
+    swap_a, swap_b = swap(0), swap(1)
+    for copy in (swap_a[0], swap_a[1], mate_pos, swap_b[0], swap_b[1], swap_a[2]):
+        copy.start()
 
     def send(stage, hop, from_piece, piece):
         ring_copy(stage, hop, from_piece, piece).start()
@@ -193,15 +192,16 @@
                 def _():
                     send(stage, hop, piece, piece)
 
-    local[0][0].wait()
-    local[0][1].wait()
-    launch(0, 0)
-    swap_a[2].start()
-    swap_a[0].wait_recv()
-    swap_a[1].wait_recv()
-    mate_pos.wait_recv()
-    launch(0, 1)
-
+    for stage in range(STAGES):
+        local[stage][0].wait()
+        local[stage][1].wait()
+        launch(stage, 0)
+    for stage, copies in enumerate((swap_a, swap_b)):
+        copies[0].wait_recv()
+        copies[1].wait_recv()
+        if stage == 0:
+            mate_pos.wait_recv()
+        launch(stage, 1)
     small[1].wait()
 
     place = jnp.concatenate([posbuf[0], posbuf[3]], axis=1)
@@ -285,56 +285,46 @@
             device_id_type=MESH,
         )
 
-    swap_b = swap(1)
     ends = (0, 3)
-
-    def first_hop_of_b():
-        for copy in swap_b:
-            copy.start()
-        local[1][0].wait()
-        local[1][1].wait()
-        launch(1, 0)
-        swap_b[0].wait_recv()
-        swap_b[1].wait_recv()
-        launch(1, 1)
 
     top[...] = jnp.full_like(top, NEG)
     total[...] = jnp.zeros_like(total)
     acc[...] = jnp.zeros_like(acc)
     take(0, 1)
-    first_hop_of_b()
+    swap_b[2].start()
+    take(1, 1)
     if hops == 8:
         take(0, 2)
-        take(1, 1)
+        take(1, 2)
         local[0][2].wait()
         swap_a[2].wait_recv()
         attend(0, 0, ends)
 
-        def early(index, carry):
-            attend(0, index)
-            stage = lax.rem(index + 1, 2)
-            take(stage, (index + 5) // 2 - stage)
+        def early(hop, carry):
+            attend(0, hop)
             return carry
 
-        lax.fori_loop(1, 5, early, 0)
+        lax.fori_loop(1, 3, early, 0)
+        take(0, 3)
         local[1][2].wait()
         swap_b[2].wait_recv()
         attend(1, 0, ends)
+        attend(1, 1)
+        take(1, 3)
 
         def late(index, carry):
-            turn, which = index // 3, lax.rem(index, 3)
-            stage = lax.rem(which + 1, 2)
-            attend(stage, stage * (2 * turn + 1 + which // 2) + (1 - stage) * (5 + turn))
-
-            @pl.when(which < 2)
+            stage = lax.rem(index, 2)
+            hop = index // 2 + 2
+            attend(stage, hop)
+
+            @pl.when((index > 1) & (index < 10))
             def _():
-                take(which, 5 + turn - which)
+                take(stage, hop + 1)
 
             return carry
 
-        lax.fori_loop(0, 9, late, 0)
+        lax.fori_loop(1, 11, late, 0)
         take(0, 8)
-        take(1, 7)
         attend(0, 8, ends, finish=True)
         attend(1, 7)
         take(1, 8)
@@ -346,7 +336,6 @@
         swap_b[2].wait_recv()
         for stage in range(STAGES):
             attend(stage, 0, ends)
-        take(1, 1)
         for hop in range(1, hops):
             for stage in range(STAGES):
                 attend(stage, hop)
@@ -379,15 +368,15 @@
 
 
 def per_device(sections, ring, queries, keys, values, token_pos, segment):
-    anywhere = pl.BlockSpec(memory_space=pl.ANY)
+    stay = pl.BlockSpec(memory_space=pltpu.HBM)
     dma = pltpu.SemaphoreType.DMA
     hops = ring // 2
     pairs = ROWS * 2 * ring * ROWS * 2 * QUERY_HEADS // 2
     return pl.pallas_call(
         functools.partial(kernel, sections, ring),
         out_shape=jax.ShapeDtypeStruct(queries.shape, jnp.bfloat16),
-        in_specs=[anywhere] * 5,
-        out_specs=anywhere,
+        in_specs=[stay] * 5,
+        out_specs=pl.BlockSpec(memory_space=pl.ANY),
         scratch_shapes=[
             pltpu.VMEM((STAGES, hops + 1, 2, 4, ROWS, HEAD_SIZE), jnp.bfloat16),
             pltpu.VMEM((STAGES, 2 * ROWS, WIDE), jnp.bfloat16),
@@ -412,12 +401,17 @@
             dma((STAGES, GROUP, 2)),
         ],
         compiler_params=pltpu.CompilerParams(
-            collective_id=0, has_side_effects=True, vmem_limit_bytes=60 * 1024 * 1024
+            collective_id=0, has_side_effects=True, vmem_limit_bytes=40 * 1024 * 1024
         ),
         cost_estimate=pl.CostEstimate(
             flops=4 * HEAD_SIZE * pairs, bytes_accessed=4 * 1024 * 1024, transcendentals=pairs
         ),
-    )(queries, keys, values, token_pos.reshape(1, ROWS), segment.reshape(-1, 128))
+    )(
+        *(
+            pltpu.with_memory_space_constraint(x, pltpu.HBM)
+            for x in (queries, keys, values, token_pos.reshape(1, ROWS), segment.reshape(-1, 128))
+        )
+    )
 
 
 def solution(mesh):

time: 79.1 us -> 77.3 us (0.977); the launches traced: 79 us -> 76 us
  Pallas kernels: 76.7 us -> 75 us
  local copies, waits for them, and re-layouts: 2.29 us -> 0.97 us
    pallas_call x1, Pallas kernels: 76.7 us -> 75 us  [per_device(): pl.pallas_call(functools.partial(kernel, sections, ring), out_shape=jax.S...]
    unnamed x1, local copies, waits for them, and re-layouts: 2.29 us -> 0.97 us
where the time goes in v3:
time: 77.3 us; the launch traced here: 76 us
  Pallas kernels  75 us (97%)
  local copies, waits for them, and re-layouts  0.97 us (1%)
    pallas_call x1, Pallas kernels, per_device(): pl.pallas_call(functools.partial(kernel, sections, ring), out_shape=jax.S...  75 us

profile of v3, /device:TPU:1, one launch (start us, length us, event | category | flops | bytes accessed | tf_op | source)
XLA Modules:
  0.0 76.0 jit_solution(10522329121515199874)
XLA Ops:
  0.0 75.0 %shard_map.55 = bf16[1,128,4096]{2,1,0:T(8,128)(2,1)S(1)} custom-call(bf16[1,128,4096]{2,1,0:T(8,128)(2,1)} %q_hbm.1, bf16[1,128,512]{2,1,0:T(8,128)(2,1)} %k_hbm.1, bf16[1,128,512]{2,1,0:T(8,128)(2,1)} %v_hbm.1, s32[1,128]{1,0:T(1,128)} %bitcast.3, s32[32,128]{1,0:T(8,128)} %bitcast.2), custom_call_target="tpu_custom_call" | custom-call | flops 8589934592 | bytes 4194304 | tf_op jit(solution)/shard_map/pallas_call | solution.py:375
  75.0 1.0 %copy.7 = bf16[1,128,4096]{2,1,0:T(8,128)(2,1)} copy(bf16[1,128,4096]{2,1,0:T(8,128)(2,1)S(1)} %shard_map.55) | data formatting | bytes 2097152

commit v4 on v3

--- a/solution.py
+++ b/solution.py
@@ -76,7 +76,7 @@
                     k_hbm.at[0, :, head_cols(half, stage)], kv.at[stage, 0, 0, 0], loc_sem.at[stage, 0]
                 ),
                 pltpu.make_async_copy(
-                    v_hbm.at[0, :, head_cols(half, stage)], kv.at[stage, 0, 1, 0], loc_sem.at[stage, 1]
+                    v_hbm.at[0, :, head_cols(half, stage)], kv.at[stage, 0, 0, 1], loc_sem.at[stage, 1]
                 ),
                 pltpu.make_async_copy(
                     q_hbm.at[0, :, wide_cols(half, stage)],
@@ -98,7 +98,7 @@
         return (
             pltpu.make_async_remote_copy(
                 k_hbm.at[0, :, head_cols(1 - half, stage)],
-                kv.at[stage, 0, 0, 3],
+                kv.at[stage, 0, 3, 0],
                 par_send.at[stage, 0],
                 par_recv.at[stage, 0],
                 device_id=(sec, mate),
@@ -106,7 +106,7 @@
             ),
             pltpu.make_async_remote_copy(
                 v_hbm.at[0, :, head_cols(1 - half, stage)],
-                kv.at[stage, 0, 1, 3],
+                kv.at[stage, 0, 3, 1],
                 par_send.at[stage, 1],
                 par_recv.at[stage, 1],
                 device_id=(sec, mate),
@@ -124,8 +124,8 @@
 
     def ring_copy(stage, hop, from_piece, piece):
         return pltpu.make_async_remote_copy(
-            kv.at[stage, hop, :, from_piece],
-            kv.at[stage, hop + 1, :, piece],
+            kv.at[stage, hop, from_piece],
+            kv.at[stage, hop + 1, piece],
             ring_send.at[stage, hop + 1, piece],
             ring_recv.at[stage, hop + 1, piece],
             device_id=toward[piece % 2],
@@ -228,8 +228,8 @@
                     bias[hop, at * ROWS : (at + 1) * ROWS, lanes] = jnp.where(allowed, 0.0, NEG)
 
         for at, piece in enumerate(pieces):
-            vt[:, at * ROWS : (at + 1) * ROWS] = jnp.transpose(kv[stage, hop, 1, piece])
-        key_rows = jnp.concatenate([kv[stage, hop, 0, piece] for piece in pieces], axis=0)
+            vt[:, at * ROWS : (at + 1) * ROWS] = jnp.transpose(kv[stage, hop, piece, 1])
+        key_rows = jnp.concatenate([kv[stage, hop, piece, 0] for piece in pieces], axis=0)
 
         def score(head):
             return lax.dot_general(
@@ -292,44 +292,65 @@
     acc[...] = jnp.zeros_like(acc)
     take(0, 1)
     swap_b[2].start()
-    take(1, 1)
     if hops == 8:
         take(0, 2)
-        take(1, 2)
+        take(1, 1)
         local[0][2].wait()
         swap_a[2].wait_recv()
         attend(0, 0, ends)
 
         def early(hop, carry):
             attend(0, hop)
+
+            @pl.when(hop == 2)
+            def _():
+                take(0, 3)
+
             return carry
 
-        lax.fori_loop(1, 3, early, 0)
-        take(0, 3)
+        lax.fori_loop(1, 4, early, 0)
+        take(1, 2)
         local[1][2].wait()
         swap_b[2].wait_recv()
         attend(1, 0, ends)
-        attend(1, 1)
-        take(1, 3)
+
+        def middle(index, carry):
+            stage = 1 - lax.rem(index, 3) * (2 - lax.rem(index, 3))
+            attend(stage, (1 - stage) * 4 + stage * (1 + index // 2 + index // 3))
+
+            @pl.when(index == 0)
+            def _():
+                take(0, 4)
+
+            @pl.when(index == 1)
+            def _():
+                take(1, 3)
+
+            return carry
+
+        lax.fori_loop(0, 4, middle, 0)
 
         def late(index, carry):
             stage = lax.rem(index, 2)
-            hop = index // 2 + 2
+            hop = 5 + index // 2 - stage
+            take(stage, hop)
             attend(stage, hop)
-
-            @pl.when((index > 1) & (index < 10))
-            def _():
-                take(stage, hop + 1)
-
             return carry
 
-        lax.fori_loop(1, 11, late, 0)
+        lax.fori_loop(0, 6, late, 0)
         take(0, 8)
         attend(0, 8, ends, finish=True)
-        attend(1, 7)
+        take(1, 7)
+
+        def rest(hop, carry):
+            attend(1, hop)
+            return carry
+
+        lax.fori_loop(7, 8, rest, 0)
         take(1, 8)
         attend(1, 8, ends, finish=True)
     else:
+        take(1, 1)
         local[0][2].wait()
         swap_a[2].wait_recv()
         local[1][2].wait()
@@ -378,7 +399,7 @@
         in_specs=[stay] * 5,
         out_specs=pl.BlockSpec(memory_space=pl.ANY),
         scratch_shapes=[
-            pltpu.VMEM((STAGES, hops + 1, 2, 4, ROWS, HEAD_SIZE), jnp.bfloat16),
+            pltpu.VMEM((STAGES, hops + 1, 4, 2, ROWS, HEAD_SIZE), jnp.bfloat16),
             pltpu.VMEM((STAGES, 2 * ROWS, WIDE), jnp.bfloat16),
             pltpu.VMEM((STAGES, 2 * ROWS, WIDE), jnp.bfloat16),
             pltpu.VMEM((1, ROWS), jnp.int32),

time: 77.3 us -> 75.4 us (0.975); the launches traced: 76 us -> 75.3 us
  no operation moved by 1% of the time
where the time goes in v4:
time: 75.4 us; the launch traced here: 75.3 us
  Pallas kernels  74.3 us (99%)
  local copies, waits for them, and re-layouts  0.97 us (1%)
    pallas_call x1, Pallas kernels, per_device(): pl.pallas_call(functools.partial(kernel, sections, ring), out_shape=jax.S...  74.3 us

profile of v4, /device:TPU:1, one launch (start us, length us, event | category | flops | bytes accessed | tf_op | source)
XLA Modules:
  0.0 75.3 jit_solution(6804711517161204313)
XLA Ops:
  0.0 74.3 %shard_map.55 = bf16[1,128,4096]{2,1,0:T(8,128)(2,1)S(1)} custom-call(bf16[1,128,4096]{2,1,0:T(8,128)(2,1)} %q_hbm.1, bf16[1,128,512]{2,1,0:T(8,128)(2,1)} %k_hbm.1, bf16[1,128,512]{2,1,0:T(8,128)(2,1)} %v_hbm.1, s32[1,128]{1,0:T(1,128)} %bitcast.3, s32[32,128]{1,0:T(8,128)} %bitcast.2), custom_call_target="tpu_custom_call" | custom-call | flops 8589934592 | bytes 4194304 | tf_op jit(solution)/shard_map/pallas_call | solution.py:396
  74.3 1.0 %copy.7 = bf16[1,128,4096]{2,1,0:T(8,128)(2,1)} copy(bf16[1,128,4096]{2,1,0:T(8,128)(2,1)S(1)} %shard_map.55) | data formatting | bytes 2097152
